TPU v7x, 32 devices: a whole 2x2x4 slice. The times are simulated.
32 devices in a mesh: grp: 2 (over y), pair: 4 (over z), aux: 2 (over x), rep: 2 (over core).
Axes of the slice: x: 2, y: 2, z: 4, core: 2. Of those that a mesh axis runs over, the one named last changes fastest.
Arguments:
- three_center: bfloat16 [5120, 4, 8000], P(('grp', 'aux', 'rep', 'pair')), parts along dimension 0, may hold values from -0.050591038 to 0.050591038
- eps_occ: float32 [8], P('grp'), parts along dimension 0, may hold values from -1.2 to -0.4
- eps_virt: float32 [16000], P(('grp', 'pair')), parts along dimension 0, may hold values from 0.2 to 3
- freq: float32 [2], P('grp'), parts along dimension 0, may hold values from 0.2 to 2
Outputs:
- polar: float32 [5120, 2560], P(('grp', 'aux', 'rep'), 'pair'), parts along dimension 0
There are 2 independent parts, one for each index of `grp`. A program takes and returns all parts, laid end to end along the dimension named above; each array names one. Nothing has to cross between parts.
All inputs are finite; a program needn't handle non-finite values.
Results may differ from a plain program's by a relative error of at most 0.0003.
Values may be sent and summed in bfloat16 or wider, within the bound.
A program may use at most 192 MiB of HBM per device.

v0:
```python
import jax
import jax.numpy as jnp
from jax import lax
from jax.sharding import PartitionSpec as P


def local(three_center, eps_occ, eps_virt, freq):
    arrived = lax.all_to_all(three_center, "pair", split_axis=2, concat_axis=0, tiled=True)
    excite = eps_virt[None, :] - eps_occ[:, None]
    weight = 2.0 * excite / (excite * excite + freq[0] * freq[0])
    height = arrived.shape[0]
    scaled = (
        (arrived.astype(jnp.float32) * weight[None, :, :]).astype(jnp.bfloat16).reshape(height, -1)
    )
    plain_rows = arrived.reshape(height, -1)
    partial_sums = lax.dot_general(
        scaled,
        lax.all_gather(plain_rows, ("aux", "rep"), axis=0, tiled=True),
        (((1,), (1,)), ((), ())),
        preferred_element_type=jnp.float32,
    )
    return lax.psum_scatter(partial_sums, "pair", scatter_dimension=1, tiled=True)


def solution(mesh):
    return jax.shard_map(
        local,
        mesh=mesh,
        in_specs=(
            P(("grp", "aux", "rep", "pair"), None, None),
            P("grp"),
            P(("grp", "pair")),
            P("grp"),
        ),
        out_specs=P(("grp", "aux", "rep"), "pair"),
        check_vma=False,
    )
```

profile of v0, /device:TPU:25, one launch (start us, length us, event | category | flops | bytes accessed | tf_op | source)
XLA Modules:
  0.0 863.6 jit_solution(16826013014737475002)
XLA Ops:
  6.5 0.0 copy-start
  6.5 0.0 all-gather.2.cloned.1.call-start
  6.5 32.8 %copy.8 = bf16[160,4,8000]{0,1,2:T(4,128)(2,1)} copy(bf16[160,4,8000]{2,1,0:T(4,128)(2,1)} %param.4) | data formatting | bytes 20480000 | tf_op args[0]
  39.3 363.2 %all_to_all.18 = bf16[160,4,8000]{0,1,2:T(4,128)(2,1)} all-to-all(bf16[160,4,8000]{0,1,2:T(4,128)(2,1)} %copy.8), channel_id=1, replica_groups=mesh['grp'=2,'pair'=4,'aux'=2,'rep'=2] {'pair'}, dimensions={2} | all-to-all | bytes 20480000 | tf_op jit(solution)/shard_map/all_to_all | solution.py:8
  402.6 35.7 %copy.9 = bf16[160,4,4,2000]{3,1,0,2:T(4,128)(2,1)} copy(bf16[160,4,4,2000]{0,1,3,2:T(4,128)(2,1)} %bitcast.4) | data formatting | bytes 20480000 | tf_op jit(solution)/shard_map/all_to_all | solution.py:8
  438.2 0.0 copy-start.2
  438.2 20.3 %all_to_all.16 = bf16[640,8000]{1,0:T(8,128)(2,1)} reshape(bf16[4,160,4,2000]{3,2,1,0:T(4,128)(2,1)} %bitcast.5) | data formatting | bytes 20480000 | tf_op jit(solution)/shard_map/all_to_all | solution.py:8
  458.6 0.0 all-gather.2.cloned.1.call-update
  458.6 0.0 reduce-scatter.2.cloned.1.call-start
  459.3 0.0 copy-done
  459.3 0.1 broadcast_reduce_fusion
  459.4 0.1 sub.24
  459.5 0.0 copy-done.2
  459.5 0.1 sub.22
  459.6 247.5 %all-gather.2.cloned.1.call-done = bf16[2560,8000]{1,0:T(8,128)(2,1)} async-done(((bf16[640,8000]{1,0:T(8,128)(2,1)}), bf16[2560,8000]{1,0:T(8,128)(2,1)}) %all-gather.2.cloned.1.call-update) | async-done | bytes 40960016 | tf_op jit(solution)/shard_map/all_gather | solution.py:18
  707.2 0.0 copy-start.1
  707.2 35.3 %fusion = f32[640,2560]{1,0:T(8,128)} fusion(bf16[2560,8000]{1,0:T(8,128)(2,1)} %all-gather.2.cloned.1.call-done, bf16[640,8000]{1,0:T(8,128)(2,1)} %all_to_all.16, f32[8000]{0:T(1024)S(1)} %add_divide_fusion), kind=kOutput, calls=%fused_computation.1 | convolution fusion | flops 26229760000 | bytes 57785600 | tf_op jit(solution)/shard_map/dot_general | solution.py:16
  742.5 0.0 reduce-scatter.2.cloned.1.call-update
  742.5 114.2 %reduce-scatter.2.cloned.1.call-done = f32[640,640]{1,0:T(8,128)} async-done(((f32[640,2560]{1,0:T(8,128)}), f32[640,640]{1,0:T(8,128)}) %reduce-scatter.2.cloned.1.call-update) | async-done | bytes 1638416 | tf_op jit(solution)/shard_map/reduce_scatter | solution.py:22
  856.7 0.0 copy-done.1
  (2 shorter events, 0.0 us)
Async XLA Ops:
  6.5 452.8 %copy-start = (f32[4]{0:T(128)S(1)}, f32[4]{0:T(128)}, u32[]{:S(2)}) copy-start(f32[4]{0:T(128)} %param.5) | copy-start | bytes 52
  6.5 700.6 %all-gather.2.cloned.1.call-start = ((), (), s32[]{:S(2)}) async-start(), calls=%async_computation.2 | async-start | bytes 51609600 | tf_op jit(solution)/shard_map/all_gather | solution.py:18
  438.2 21.3 %copy-start.2 = (f32[2000]{0:T(1024)S(1)}, f32[2000]{0:T(1024)}, u32[]{:S(2)}) copy-start(f32[2000]{0:T(1024)} %param.6) | copy-start | bytes 24004
  458.6 398.1 %reduce-scatter.2.cloned.1.call-start = ((), (), s32[]{:S(2)}) async-start(), calls=%async_computation.3 | async-start | bytes 8192000 | tf_op jit(solution)/shard_map/reduce_scatter | solution.py:22
  707.2 149.5 %copy-start.1 = (f32[4]{0:T(128)S(1)}, f32[4]{0:T(128)}, u32[]{:S(2)}) copy-start(f32[4]{0:T(128)} %param.5) | copy-start | bytes 52
Sparse Core Ops, SparseCore 0:
  458.7 248.4 all-gather.1
  742.7 114.0 reduce-scatter.1
where the time goes:
time: 869 us; the launch traced here: 864 us
  blocking collectives  363 us (42%)
  waiting for transfers between devices  362 us (42%)
  local copies, waits for them, and re-layouts  89.1 us (10%)
  matrix products  35.3 us (4%)
  between operations  14.1 us (2%)
    all_to_all x1, blocking collectives, local(): lax.all_to_all(three_center, 'pair', split_axis=2, concat_axis=0, tiled=T...  363 us
    all_gather x1, waiting for transfers between devices, local(): lax.all_gather(plain_rows, ('aux', 'rep'), axis=0, tiled=True)  248 us
    reduce_scatter x1, waiting for transfers between devices, local(): lax.psum_scatter(partial_sums, 'pair', scatter_dimension=1, tiled=True)  114 us
    all_to_all x2, local copies, waits for them, and re-layouts, local(): lax.all_to_all(three_center, 'pair', split_axis=2, concat_axis=0, tiled=T...  56 us
    dot_general x1, matrix products, local(): lax.dot_general(scaled, lax.all_gather(plain_rows, ('aux', 'rep'), axis=0...  35.3 us
    unnamed x7, local copies, waits for them, and re-layouts  32.8 us
  transfers between devices with their start and end apart: 2, of which 2 were waited for; matrix products, arithmetic and copies ran while one was open for 0% of the time, Pallas kernels for 0%

commit v1 on v0

v1 whole, which is shorter than its diff:
```python
import functools
import jax
import jax.numpy as jnp
from jax import lax
from jax.experimental import pallas as pl
from jax.experimental.pallas import tpu as pltpu
from jax.sharding import PartitionSpec as P

MESH = pl.DeviceIdType.MESH


def gather_kernel(sizes, x_ref, g_ref, zs, zr, xs, xr, cs, cr, ls):
    n_pair, n_aux, n_rep, chunks, rows = sizes
    z = lax.axis_index("pair")
    a = lax.axis_index("aux")
    r = lax.axis_index("rep")
    step = rows // chunks

    def turn(i, k, n):
        return lax.rem(i + k, n)

    peers = (
        [("pair", turn(z, k, n_pair)) for k in range(1, n_pair)]
        + [("aux", turn(a, k, n_aux)) for k in range(1, n_aux)]
        + [("rep", turn(r, k, n_rep)) for k in range(1, n_rep)]
    )
    barrier = pltpu.get_barrier_semaphore()
    for name, index in peers:
        pl.semaphore_signal(barrier, inc=1, device_id={name: index}, device_id_type=MESH)
    pl.semaphore_wait(barrier, len(peers))

    def block(aux, rep, pair, c):
        return g_ref.at[aux, rep, pair, pl.ds(c * step, step)]

    def z_copy(c, k, sending):
        to = turn(z, k, n_pair)
        src = turn(z, n_pair - k, n_pair)
        return pltpu.make_async_remote_copy(
            src_ref=x_ref.at[to, pl.ds(c * step, step)],
            dst_ref=block(a, r, z if sending else src, c),
            send_sem=zs.at[c, k],
            recv_sem=zr.at[c, k],
            device_id={"pair": to},
            device_id_type=MESH,
        )

    def x_copy(c, k, j, sending):
        pair = turn(z, n_pair - j, n_pair)
        mine = a if sending else turn(a, n_aux - k, n_aux)
        if j == 0 and sending:
            src = x_ref.at[z, pl.ds(c * step, step)]
        else:
            src = block(mine, r, pair, c)
        return pltpu.make_async_remote_copy(
            src_ref=src,
            dst_ref=block(mine, r, pair, c),
            send_sem=xs.at[c, k, j],
            recv_sem=xr.at[c, k, j],
            device_id={"aux": turn(a, k, n_aux)},
            device_id_type=MESH,
        )

    def c_copy(c, m, k, j, sending):
        pair = turn(z, n_pair - j, n_pair)
        aux = turn(a, n_aux - k, n_aux)
        rep = r if sending else turn(r, n_rep - m, n_rep)
        if j == 0 and k == 0 and sending:
            src = x_ref.at[z, pl.ds(c * step, step)]
        else:
            src = block(aux, rep, pair, c)
        return pltpu.make_async_remote_copy(
            src_ref=src,
            dst_ref=block(aux, rep, pair, c),
            send_sem=cs.at[c, m, k, j],
            recv_sem=cr.at[c, m, k, j],
            device_id={"rep": turn(r, m, n_rep)},
            device_id_type=MESH,
        )

    for c in range(chunks):
        for k in range(1, n_pair):
            z_copy(c, k, True).start()
    own = pltpu.make_async_copy(x_ref.at[z], g_ref.at[a, r, z], ls)
    own.start()

    def arrived(c, j):
        if j:
            z_copy(c, j, False).wait_recv()
        for k in range(1, n_aux):
            x_copy(c, k, j, True).start()
        for m in range(1, n_rep):
            c_copy(c, m, 0, j, True).start()

    def crossed(c, j):
        for k in range(1, n_aux):
            x_copy(c, k, j, False).wait_recv()
            for m in range(1, n_rep):
                c_copy(c, m, k, j, True).start()

    for c in range(chunks):
        arrived(c, 0)
    for c in range(chunks):
        for j in range(1, n_pair):
            arrived(c, j)
        crossed(c, 0)
        if c:
            for j in range(1, n_pair):
                crossed(c - 1, j)
    for j in range(1, n_pair):
        crossed(chunks - 1, j)

    own.wait()
    for c in range(chunks):
        for k in range(1, n_pair):
            z_copy(c, k, True).wait_send()
        for j in range(n_pair):
            for k in range(1, n_aux):
                x_copy(c, k, j, True).wait_send()
            for m in range(1, n_rep):
                for k in range(n_aux):
                    c_copy(c, m, k, j, True).wait_send()
                    c_copy(c, m, k, j, False).wait_recv()


def gather(pieces, n_aux, n_rep):
    n_pair, rows, width = pieces.shape
    chunks = 5 if rows % 80 == 0 else 1
    sizes = (n_pair, n_aux, n_rep, chunks, rows)
    dma = pltpu.SemaphoreType.DMA
    return pl.pallas_call(
        functools.partial(gather_kernel, sizes),
        out_shape=jax.ShapeDtypeStruct((n_aux, n_rep, n_pair, rows, width), pieces.dtype),
        in_specs=[pl.BlockSpec(memory_space=pl.ANY)],
        out_specs=pl.BlockSpec(memory_space=pl.ANY),
        scratch_shapes=[
            dma((chunks, n_pair)),
            dma((chunks, n_pair)),
            dma((chunks, n_aux, n_pair)),
            dma((chunks, n_aux, n_pair)),
            dma((chunks, n_rep, n_aux, n_pair)),
            dma((chunks, n_rep, n_aux, n_pair)),
            dma,
        ],
        compiler_params=pltpu.CompilerParams(collective_id=0, has_side_effects=True),
    )(pieces)


def local(mesh, three_center, eps_occ, eps_virt, freq):
    n_pair, n_aux, n_rep = (mesh.shape[name] for name in ("pair", "aux", "rep"))
    rows, n_occ, n_virt = three_center.shape
    parts = n_pair // n_occ
    width = n_virt // parts
    every_virt = lax.all_gather(eps_virt, "pair", axis=0, tiled=True)
    pieces = three_center.reshape(rows, n_pair, width).transpose(1, 0, 2)
    gathered = gather(pieces, n_aux, n_rep)

    z = lax.axis_index("pair")
    virt = lax.dynamic_slice_in_dim(every_virt, lax.rem(z, parts) * width, width)
    occ = lax.dynamic_index_in_dim(eps_occ, z // parts, keepdims=False)
    excite = virt - occ
    weight = 2.0 * excite / (excite * excite + freq[0] * freq[0])
    plain = gathered.reshape(n_aux * n_rep, n_pair * rows, width)
    mine = lax.axis_index("aux") * n_rep + lax.axis_index("rep")
    own = lax.dynamic_index_in_dim(plain, mine, keepdims=False)
    scaled = (own.astype(jnp.float32) * weight[None, :]).astype(jnp.bfloat16)
    partial_sums = lax.dot_general(
        scaled,
        plain.reshape(-1, width),
        (((1,), (1,)), ((), ())),
        preferred_element_type=jnp.float32,
    )
    return lax.psum_scatter(partial_sums, "pair", scatter_dimension=1, tiled=True)


def solution(mesh):
    return jax.shard_map(
        functools.partial(local, mesh),
        mesh=mesh,
        in_specs=(
            P(("grp", "aux", "rep", "pair"), None, None),
            P("grp"),
            P(("grp", "pair")),
            P("grp"),
        ),
        out_specs=P(("grp", "aux", "rep"), "pair"),
        check_vma=False,
    )
```

time: 869 us -> 470 us (0.54)
  blocking collectives: 363 us -> 12 us
  Pallas kernels: 0 us -> 276 us
  waiting for transfers between devices: 362 us -> 119 us
  local copies, waits for them, and re-layouts: 89.1 us -> 10.5 us
    all_to_all x1 -> x0, blocking collectives: 363 us -> none  [local(): lax.all_to_all(three_center, 'pair', split_axis=2, concat_axis=0, tiled=T...]
    pallas_call x0 -> x1, Pallas kernels: none -> 276 us  [gather(): pl.pallas_call(functools.partial(gather_kernel, sizes), out_shape=jax.Sha...]
    all_gather x1 -> x0, waiting for transfers between devices: 248 us -> none  [local(): lax.all_gather(plain_rows, ('aux', 'rep'), axis=0, tiled=True)]
    all_to_all x2 -> x0, local copies, waits for them, and re-layouts: 56 us -> none  [local(): lax.all_to_all(three_center, 'pair', split_axis=2, concat_axis=0, tiled=T...]
    unnamed x7 -> x10, local copies, waits for them, and re-layouts: 32.8 us -> 9.79 us
    unnamed x0 -> x1, blocking collectives: none -> 12 us
  transfers between devices with their start and end apart: 2 -> 1, of which waited for: 2 -> 1; matrix products, arithmetic and copies ran while one was open for 0% -> 0% of each run, Pallas kernels for 0% -> 0%
where the time goes in v1:
time: 470 us; the launch traced here: 468 us
  Pallas kernels  276 us (59%)
  waiting for transfers between devices  119 us (25%)
  matrix products  35.6 us (8%)
  between operations  14.8 us (3%)
  blocking collectives  12 us (3%)
  local copies, waits for them, and re-layouts  10.5 us (2%)
    pallas_call x1, Pallas kernels, gather(): pl.pallas_call(functools.partial(gather_kernel, sizes), out_shape=jax.Sha...  276 us
    reduce_scatter x1, waiting for transfers between devices, local(): lax.psum_scatter(partial_sums, 'pair', scatter_dimension=1, tiled=True)  119 us
    dot_general x1, matrix products, local(): lax.dot_general(scaled, plain.reshape(-1, width), (((1,), (1,)), ((), ())...  35.6 us
    unnamed x1, blocking collectives  12 us
    unnamed x10, local copies, waits for them, and re-layouts  9.79 us
  transfers between devices with their start and end apart: 1, of which 1 were waited for; matrix products, arithmetic and copies ran while one was open for 0% of the time, Pallas kernels for 0%

profile of v1, /device:TPU:25, one launch (start us, length us, event | category | flops | bytes accessed | tf_op | source)
XLA Modules:
  0.0 467.9 jit_solution(3325169330112399547)
XLA Ops:
  6.5 0.0 reduce-scatter.2.cloned.1.call-start
  6.5 8.9 %copy.7 = bf16[160,4,8000]{2,0,1:T(8,128)(2,1)} copy(bf16[160,4,8000]{2,1,0:T(4,128)(2,1)} %param.4) | data formatting | bytes 20480000 | tf_op args[0]
  15.4 0.0 copy-start.2
  15.4 0.0 copy-start
  15.4 0.0 copy-start.1
  15.4 275.7 %shard_map.46 = bf16[2,2,4,160,8000]{4,3,2,1,0:T(8,128)(2,1)} custom-call(bf16[4,160,8000]{2,1,0:T(8,128)(2,1)} %bitcast.14), custom_call_target="tpu_custom_call" | custom-call | tf_op jit(solution)/shard_map/pallas_call | solution.py:130
  291.1 0.0 copy-done.2
  291.1 0.6 dynamic-slice
  292.4 0.0 copy-done
  292.4 0.3 dynamic-update-slice
  292.7 12.0 %all-reduce = f32[8000]{0:T(1024)S(1)} all-reduce(f32[8000]{0:T(1024)S(1)} %dynamic-update-slice), channel_id=1, replica_groups=mesh['grp'=2,'pair'=4,'aux'=2,'rep'=2] {'pair'}, use_global_device_ids=true, to_apply=%add | all-reduce | flops 8000 | bytes 64000
  305.3 0.0 copy-done.1
  305.3 0.7 dynamic_slice.10
  306.0 0.7 add_divide_fusion
  306.7 35.6 %fusion.1 = f32[640,2560]{1,0:T(8,128)} fusion(bf16[2560,8000]{1,0:T(8,128)(2,1)} %bitcast.12, f32[8000]{0:T(1024)S(1)} %add_divide_fusion, bf16[4,640,8000]{2,1,0:T(8,128)(2,1)} %bitcast.13, s32[]{:T(128)S(6)} %select_n.12), kind=kOutput, calls=%fused_computation.2 | convolution fusion | flops 26229760000 | bytes 58195204 | tf_op jit(solution)/shard_map/dot_general | solution.py:166
  342.3 0.0 reduce-scatter.2.cloned.1.call-update
  342.3 118.7 %reduce-scatter.2.cloned.1.call-done = f32[640,640]{1,0:T(8,128)} async-done(((f32[640,2560]{1,0:T(8,128)}), f32[640,640]{1,0:T(8,128)}) %reduce-scatter.2.cloned.1.call-update) | async-done | bytes 1638416 | tf_op jit(solution)/shard_map/reduce_scatter | solution.py:172
  (1 shorter events, 0.0 us)
Async XLA Ops:
  6.5 454.5 %reduce-scatter.2.cloned.1.call-start = ((), (), s32[]{:S(2)}) async-start(), calls=%async_computation.1 | async-start | bytes 8192000 | tf_op jit(solution)/shard_map/reduce_scatter | solution.py:172
  15.4 275.7 %copy-start.2 = (u32[32]{0:T(128)S(1)}, u32[32]{0:T(128)}, u32[]{:S(2)}) copy-start(u32[32]{0:T(128)} %constant.41) | copy-start | bytes 388
  15.4 277.0 %copy-start = (f32[2000]{0:T(1024)S(1)}, f32[2000]{0:T(1024)}, u32[]{:S(2)}) copy-start(f32[2000]{0:T(1024)} %param.6) | copy-start | bytes 24004
  15.4 289.9 %copy-start.1 = (f32[4]{0:T(128)S(1)}, f32[4]{0:T(128)}, u32[]{:S(2)}) copy-start(f32[4]{0:T(128)} %param.5) | copy-start | bytes 52
Sparse Core Ops, SparseCore 0:
  342.5 118.5 reduce-scatter.1

commit v2 on v1

--- a/solution.py
+++ b/solution.py
@@ -145,8 +145,251 @@
     )(pieces)
 
 
+def fused_kernel(sizes, x_ref, w_ref, o_ref, g, p, s1, s2, lhs, zs, zr, xs, xr, cs, cr, ls, s1s, s1r, s2s, s2r):
+    n_pair, n_aux, n_rep, chunks, step, width = sizes
+    z = lax.axis_index("pair")
+    a = lax.axis_index("aux")
+    r = lax.axis_index("rep")
+    mine = a * n_rep + r
+    tall = n_pair * step
+
+    def turn(i, k, n):
+        return lax.rem(i + k, n)
+
+    peers = (
+        [("pair", turn(z, k, n_pair)) for k in range(1, n_pair)]
+        + [("aux", turn(a, k, n_aux)) for k in range(1, n_aux)]
+        + [("rep", turn(r, k, n_rep)) for k in range(1, n_rep)]
+    )
+    barrier = pltpu.get_barrier_semaphore()
+    for name, index in peers:
+        pl.semaphore_signal(barrier, inc=1, device_id={name: index}, device_id_type=MESH)
+    pl.semaphore_wait(barrier, len(peers))
+
+    def send(src, dst, send_sem, recv_sem, name, to):
+        return pltpu.make_async_remote_copy(
+            src_ref=src,
+            dst_ref=dst,
+            send_sem=send_sem,
+            recv_sem=recv_sem,
+            device_id={name: to},
+            device_id_type=MESH,
+        )
+
+    def z_copy(c, k, sending):
+        to = turn(z, k, n_pair)
+        pair = z if sending else turn(z, n_pair - k, n_pair)
+        return send(x_ref.at[to, c], g.at[c, mine, pair], zs.at[c, k], zr.at[c, k], "pair", to)
+
+    def x_copy(c, k, j, sending):
+        pair = turn(z, n_pair - j, n_pair)
+        aux = a if sending else turn(a, n_aux - k, n_aux)
+        dst = g.at[c, aux * n_rep + r, pair]
+        src = x_ref.at[z, c] if j == 0 and sending else dst
+        return send(src, dst, xs.at[c, k, j], xr.at[c, k, j], "aux", turn(a, k, n_aux))
+
+    def c_copy(c, m, k, j, sending):
+        pair = turn(z, n_pair - j, n_pair)
+        aux = turn(a, n_aux - k, n_aux)
+        rep = r if sending else turn(r, n_rep - m, n_rep)
+        dst = g.at[c, aux * n_rep + rep, pair]
+        src = x_ref.at[z, c] if j == 0 and k == 0 and sending else dst
+        return send(src, dst, cs.at[c, m, k, j], cr.at[c, m, k, j], "rep", turn(r, m, n_rep))
+
+    def start_z(c):
+        if c < chunks:
+            for k in range(1, n_pair):
+                z_copy(c, k, True).start()
+
+    def arrived(c, j):
+        if j:
+            z_copy(c, j, False).wait_recv()
+        for k in range(1, n_aux):
+            x_copy(c, k, j, True).start()
+        for m in range(1, n_rep):
+            c_copy(c, m, 0, j, True).start()
+
+    def crossed(c, j):
+        for k in range(1, n_aux):
+            x_copy(c, k, j, False).wait_recv()
+            for m in range(1, n_rep):
+                c_copy(c, m, k, j, True).start()
+
+    def complete(c):
+        for j in range(n_pair):
+            for m in range(1, n_rep):
+                for k in range(n_aux):
+                    c_copy(c, m, k, j, False).wait_recv()
+
+    odd = lax.rem(z, 2)
+    near = z + 1 - 2 * odd
+    far = lax.rem(z + 2, 4)
+    half = lax.div(z, 2)
+
+    def span(c):
+        return pl.ds(c * c, 2 * c + 1)
+
+    def first(c, b):
+        block = 1 - odd + 2 * b
+        return send(p.at[block, span(c)], s1.at[b, span(c)], s1s.at[c, b], s1r.at[c, b], "pair", near)
+
+    def second(c):
+        return send(p.at[far, span(c)], s2.at[span(c)], s2s.at[c], s2r.at[c], "pair", far)
+
+    def scale(c):
+        own = g[c, mine].reshape(tall, width).astype(jnp.float32)
+        lhs[...] = (own * w_ref[...]).astype(jnp.bfloat16)
+
+    def tiles(c, t):
+        @pl.loop(0, n_aux * n_rep // 2)
+        def _(h):
+            rhs = g[c, pl.ds(2 * h, 2)].reshape(2 * tall, width)
+            got = lax.dot_general(
+                lhs[...], rhs, (((1,), (1,)), ((), ())), preferred_element_type=jnp.float32
+            )
+            p[2 * h, t] = got[:, :tall]
+            p[2 * h + 1, t] = got[:, tall:]
+
+    def compute(c):
+        if c:
+            @pl.loop(0, c)
+            def _(i):
+                scale(i)
+                tiles(c, c * c + i)
+
+        scale(c)
+
+        @pl.loop(0, c + 1)
+        def _(i):
+            tiles(i, c * c + c + i)
+
+        for b in range(2):
+            first(c, b).start()
+
+    def halve(c):
+        for b in range(2):
+            first(c, b).wait_recv()
+
+        @pl.loop(c * c, (c + 1) * (c + 1))
+        def _(t):
+            p[far, t] += s1[1 - half, t]
+
+        second(c).start()
+
+        @pl.loop(c * c, (c + 1) * (c + 1))
+        def _(t):
+            p[z, t] += s1[half, t]
+
+    def finish(c):
+        second(c).wait_recv()
+        if c:
+            @pl.loop(0, c)
+            def _(i):
+                o_ref[i, c] = p[z, c * c + i] + s2[c * c + i]
+
+        @pl.loop(0, c + 1)
+        def _(i):
+            o_ref[c, i] = p[z, c * c + c + i] + s2[c * c + c + i]
+
+    start_z(0)
+    start_z(1)
+    own = pltpu.make_async_copy(x_ref.at[z], g.at[:, mine, z], ls)
+    own.start()
+    for c in range(chunks):
+        arrived(c, 0)
+    own.wait()
+    for c in range(chunks + 1):
+        if c < chunks:
+            for j in range(1, n_pair):
+                arrived(c, j)
+            start_z(c + 2)
+        if c:
+            for j in range(n_pair):
+                crossed(c - 1, j)
+            complete(c - 1)
+            compute(c - 1)
+        if c > 1:
+            halve(c - 2)
+        if c > 2:
+            finish(c - 3)
+    halve(chunks - 1)
+    finish(chunks - 2)
+    finish(chunks - 1)
+
+    for c in range(chunks):
+        second(c).wait_send()
+        for b in range(2):
+            first(c, b).wait_send()
+        for k in range(1, n_pair):
+            z_copy(c, k, True).wait_send()
+        for j in range(n_pair):
+            for k in range(1, n_aux):
+                x_copy(c, k, j, True).wait_send()
+            for m in range(1, n_rep):
+                for k in range(n_aux):
+                    c_copy(c, m, k, j, True).wait_send()
+
+
+def fused(pieces, weight, n_aux, n_rep):
+    n_pair, chunks, step, width = pieces.shape
+    tall = n_pair * step
+    groups = n_aux * n_rep
+    sizes = (n_pair, n_aux, n_rep, chunks, step, width)
+    dma = pltpu.SemaphoreType.DMA
+    return pl.pallas_call(
+        functools.partial(fused_kernel, sizes),
+        out_shape=jax.ShapeDtypeStruct((chunks, chunks, tall, tall), jnp.float32),
+        in_specs=[pl.BlockSpec(memory_space=pl.ANY), pl.BlockSpec(memory_space=pltpu.VMEM)],
+        out_specs=pl.BlockSpec(memory_space=pltpu.VMEM),
+        scratch_shapes=[
+            pltpu.VMEM((chunks, groups, n_pair, step, width), jnp.bfloat16),
+            pltpu.VMEM((groups, chunks * chunks, tall, tall), jnp.float32),
+            pltpu.VMEM((2, chunks * chunks, tall, tall), jnp.float32),
+            pltpu.VMEM((chunks * chunks, tall, tall), jnp.float32),
+            pltpu.VMEM((tall, width), jnp.bfloat16),
+            dma((chunks, n_pair)),
+            dma((chunks, n_pair)),
+            dma((chunks, n_aux, n_pair)),
+            dma((chunks, n_aux, n_pair)),
+            dma((chunks, n_rep, n_aux, n_pair)),
+            dma((chunks, n_rep, n_aux, n_pair)),
+            dma,
+            dma((chunks, 2)),
+            dma((chunks, 2)),
+            dma((chunks,)),
+            dma((chunks,)),
+        ],
+        compiler_params=pltpu.CompilerParams(
+            collective_id=1, has_side_effects=True, vmem_limit_bytes=60 * 2**20
+        ),
+    )(pieces, weight)
+
+
 def local(mesh, three_center, eps_occ, eps_virt, freq):
     n_pair, n_aux, n_rep = (mesh.shape[name] for name in ("pair", "aux", "rep"))
+    rows, n_occ, n_virt = three_center.shape
+    if n_pair == n_occ == n_aux * n_rep == 4 and rows % 32 == 0:
+        return whole_kernel(n_aux, n_rep, three_center, eps_occ, eps_virt, freq)
+    return staged(n_pair, n_aux, n_rep, three_center, eps_occ, eps_virt, freq)
+
+
+def whole_kernel(n_aux, n_rep, three_center, eps_occ, eps_virt, freq):
+    rows, n_pair, n_virt = three_center.shape
+    pad = -n_virt % 128
+    chunks = rows // 32
+    virt = lax.all_gather(eps_virt, "pair", axis=0, tiled=True)
+    occ = lax.dynamic_index_in_dim(eps_occ, lax.axis_index("pair"), keepdims=False)
+    excite = virt - occ
+    weight = 2.0 * excite / (excite * excite + freq[0] * freq[0])
+    weight = jnp.pad(weight, (0, pad))[None, :]
+    pieces = jnp.pad(three_center.transpose(1, 0, 2), ((0, 0), (0, 0), (0, pad)))
+    pieces = pieces.reshape(n_pair, chunks, 32, n_virt + pad)
+    out = fused(pieces, weight, n_aux, n_rep)
+    out = out.reshape(chunks, chunks, n_pair, 32, n_pair, 32)
+    return out.transpose(2, 0, 3, 4, 1, 5).reshape(n_pair * rows, n_pair * rows)
+
+
+def staged(n_pair, n_aux, n_rep, three_center, eps_occ, eps_virt, freq):
     rows, n_occ, n_virt = three_center.shape
     parts = n_pair // n_occ
     width = n_virt // parts

time: 470 us -> 425 us (0.904)
  waiting for transfers between devices: 119 us -> 0 us
  Pallas kernels: 276 us -> 365 us
  matrix products: 35.6 us -> 0 us
  local copies, waits for them, and re-layouts: 10.5 us -> 45 us
  between operations: 14.8 us -> 1.36 us
    reduce_scatter x1 -> x0, waiting for transfers between devices: 119 us -> none  [local(): lax.psum_scatter(partial_sums, 'pair', scatter_dimension=1, tiled=True)]
    pallas_call x1, Pallas kernels: 276 us -> 365 us  [fused(): pl.pallas_call(functools.partial(fused_kernel, sizes), out_shape=jax.Shap...]
    dot_general x1 -> x0, matrix products: 35.6 us -> none  [local(): lax.dot_general(scaled, plain.reshape(-1, width), (((1,), (1,)), ((), ())...]
    reshape x0 -> x3, local copies, waits for them, and re-layouts: none -> 25.5 us  [the longest x2 18 us: whole_kernel(): out = out.reshape(chunks, chunks, n_pair, 32, n_pair, 32)]
    pad x0 -> x2, local copies, waits for them, and re-layouts: none -> 8.57 us  [the longest x1 8.57 us: whole_kernel(): jnp.pad(three_center.transpose(1, 0, 2), ((0, 0), (0, 0), (0, pad)))]
  transfers between devices with their start and end apart: 1 -> 0, of which waited for: 1 -> 0; matrix products, arithmetic and copies ran while one was open for 0% -> 0% of each run, Pallas kernels for 0% -> 0%
where the time goes in v2:
time: 425 us; the launch traced here: 424 us
  Pallas kernels  365 us (86%)
  local copies, waits for them, and re-layouts  45 us (11%)
  blocking collectives  12 us (3%)
    pallas_call x1, Pallas kernels, fused(): pl.pallas_call(functools.partial(fused_kernel, sizes), out_shape=jax.Shap...  365 us
    reshape x2, local copies, waits for them, and re-layouts, whole_kernel(): out = out.reshape(chunks, chunks, n_pair, 32, n_pair, 32)  18 us
    unnamed x1, blocking collectives  12 us
    unnamed x10, local copies, waits for them, and re-layouts  9.72 us
    pad x1, local copies, waits for them, and re-layouts, whole_kernel(): jnp.pad(three_center.transpose(1, 0, 2), ((0, 0), (0, 0), (0, pad)))  8.57 us

profile of v2, /device:TPU:25, one launch (start us, length us, event | category | flops | bytes accessed | tf_op | source)
XLA Modules:
  0.0 424.2 jit_solution(2853725200078998570)
XLA Ops:
  0.0 8.8 %copy.9 = bf16[4,160,8000]{2,1,0:T(8,128)(2,1)} copy(bf16[4,160,8000]{2,0,1:T(4,128)(2,1)} %bitcast.12) | data formatting | bytes 20480000
  8.8 0.0 copy-start.2
  8.8 0.0 copy-start
  8.8 0.0 copy-start.1
  8.8 8.6 %pad.8.clone = bf16[4,160,8064]{2,1,0:T(8,128)(2,1)} pad(bf16[4,160,8000]{2,1,0:T(8,128)(2,1)} %copy.9, bf16[]{:T(256)} %constant.11.clone.1), padding=0_0x0_0x0_64 | pad | bytes 20561922 | tf_op jit(solution)/shard_map/jit(_pad)/pad | solution.py:385
  17.4 0.0 copy-done.2
  17.4 0.6 dynamic-slice
  18.6 0.0 copy-done
  18.6 0.3 dynamic-update-slice
  19.0 12.0 %all-reduce.2 = f32[8000]{0:T(1024)S(1)} all-reduce(f32[8000]{0:T(1024)S(1)} %dynamic-update-slice), channel_id=1, replica_groups=mesh['grp'=2,'pair'=4,'aux'=2,'rep'=2] {'pair'}, use_global_device_ids=true, to_apply=%add.2 | all-reduce | flops 8000 | bytes 64000
  31.6 0.0 copy-done.1
  31.6 0.6 dynamic_slice.4
  32.2 0.6 add_divide_fusion
  32.9 0.6 broadcast_in_dim.3.w_ref
  33.5 365.2 %shard_map.46 = f32[5,5,128,128]{3,2,1,0:T(8,128)} custom-call(bf16[4,5,32,8064]{3,2,1,0:T(8,128)(2,1)} %bitcast.11, f32[1,8064]{1,0:T(1,128)} %broadcast_in_dim.3.w_ref), custom_call_target="tpu_custom_call" | custom-call | tf_op jit(solution)/shard_map/pallas_call | solution.py:339
  398.7 6.3 %reshape.11 = f32[5,5,4,32,4,32]{5,4,3,2,1,0:T(4,128)} reshape(f32[5,5,128,128]{3,2,1,0:T(8,128)} %shard_map.46) | data formatting | bytes 3276800 | tf_op jit(solution)/shard_map/reshape | solution.py:388
  405.0 11.8 %copy.11 = f32[5,5,4,32,4,32]{5,1,4,3,0,2:T(8,128)} copy(f32[5,5,4,32,4,32]{5,4,3,2,1,0:T(4,128)} %reshape.11) | data formatting | bytes 3276800 | tf_op jit(solution)/shard_map/reshape | solution.py:388
  416.7 7.5 %reshape.12 = f32[640,640]{1,0:T(8,128)} reshape(f32[4,5,32,4,5,32]{5,4,3,2,1,0:T(8,128)} %bitcast.10) | data formatting | bytes 3276800 | tf_op jit(solution)/shard_map/reshape | solution.py:389
  (2 shorter events, 0.0 us)
Async XLA Ops:
  8.8 8.6 %copy-start.2 = (u32[32]{0:T(128)S(1)}, u32[32]{0:T(128)}, u32[]{:S(2)}) copy-start(u32[32]{0:T(128)} %constant.25) | copy-start | bytes 388
  8.8 9.8 %copy-start = (f32[2000]{0:T(1024)S(1)}, f32[2000]{0:T(1024)}, u32[]{:S(2)}) copy-start(f32[2000]{0:T(1024)} %param.6) | copy-start | bytes 24004
  8.8 22.8 %copy-start.1 = (f32[4]{0:T(128)S(1)}, f32[4]{0:T(128)}, u32[]{:S(2)}) copy-start(f32[4]{0:T(128)} %param.5) | copy-start | bytes 52

commit v3 on v2

--- a/solution.py
+++ b/solution.py
@@ -145,7 +145,10 @@
     )(pieces)
 
 
-def fused_kernel(sizes, x_ref, w_ref, o_ref, g, p, s1, s2, lhs, zs, zr, xs, xr, cs, cr, ls, s1s, s1r, s2s, s2r):
+def fused_kernel(
+    sizes, x_ref, occ_ref, virt_ref, freq_ref, o_ref, g, p, s1, s2, lhs, levels, w_ref,
+    zs, zr, xs, xr, cs, cr, ls, s1s, s1r, s2s, s2r, es, er,
+):
     n_pair, n_aux, n_rep, chunks, step, width = sizes
     z = lax.axis_index("pair")
     a = lax.axis_index("aux")
@@ -236,6 +239,20 @@
     def second(c):
         return send(p.at[far, span(c)], s2.at[span(c)], s2s.at[c], s2r.at[c], "pair", far)
 
+    def e_copy(k, sending):
+        pair = z if sending else turn(z, n_pair - k, n_pair)
+        return send(virt_ref, levels.at[pair], es.at[k], er.at[k], "pair", turn(z, k, n_pair))
+
+    def weigh():
+        levels[z] = virt_ref[...]
+        for k in range(1, n_pair):
+            e_copy(k, False).wait_recv()
+        freq = freq_ref[0]
+        piece = virt_ref.shape[1]
+        for k in range(n_pair):
+            excite = levels[k] - occ_ref[z]
+            w_ref[:, k * piece : (k + 1) * piece] = 2.0 * excite / (excite * excite + freq * freq)
+
     def scale(c):
         own = g[c, mine].reshape(tall, width).astype(jnp.float32)
         lhs[...] = (own * w_ref[...]).astype(jnp.bfloat16)
@@ -280,23 +297,35 @@
         def _(t):
             p[z, t] += s1[half, t]
 
+    def place(c1, c2, t):
+        done = p[z, t] + s2[t]
+        for i in range(n_pair):
+            row = pl.multiple_of(i * chunks * step + c1 * step, step)
+            for j in range(n_pair):
+                column = (j * chunks + c2) * step
+                o_ref[pl.ds(row, step), column : column + step] = done[
+                    i * step : (i + 1) * step, j * step : (j + 1) * step
+                ]
+
     def finish(c):
         second(c).wait_recv()
         if c:
             @pl.loop(0, c)
             def _(i):
-                o_ref[i, c] = p[z, c * c + i] + s2[c * c + i]
-
-        @pl.loop(0, c + 1)
-        def _(i):
-            o_ref[c, i] = p[z, c * c + c + i] + s2[c * c + c + i]
-
+                place(i, c, c * c + i)
+
+        for i in range(c + 1):
+            place(c, i, c * c + c + i)
+
+    for k in range(1, n_pair):
+        e_copy(k, True).start()
     start_z(0)
     start_z(1)
     own = pltpu.make_async_copy(x_ref.at[z], g.at[:, mine, z], ls)
     own.start()
     for c in range(chunks):
         arrived(c, 0)
+    weigh()
     own.wait()
     for c in range(chunks + 1):
         if c < chunks:
@@ -316,6 +345,8 @@
     finish(chunks - 2)
     finish(chunks - 1)
 
+    for k in range(1, n_pair):
+        e_copy(k, True).wait_send()
     for c in range(chunks):
         second(c).wait_send()
         for b in range(2):
@@ -330,7 +361,7 @@
                     c_copy(c, m, k, j, True).wait_send()
 
 
-def fused(pieces, weight, n_aux, n_rep):
+def fused(pieces, eps_occ, eps_virt, freq, n_aux, n_rep):
     n_pair, chunks, step, width = pieces.shape
     tall = n_pair * step
     groups = n_aux * n_rep
@@ -338,8 +369,13 @@
     dma = pltpu.SemaphoreType.DMA
     return pl.pallas_call(
         functools.partial(fused_kernel, sizes),
-        out_shape=jax.ShapeDtypeStruct((chunks, chunks, tall, tall), jnp.float32),
-        in_specs=[pl.BlockSpec(memory_space=pl.ANY), pl.BlockSpec(memory_space=pltpu.VMEM)],
+        out_shape=jax.ShapeDtypeStruct((chunks * tall, chunks * tall), jnp.float32),
+        in_specs=[
+            pl.BlockSpec(memory_space=pl.ANY),
+            pl.BlockSpec(memory_space=pltpu.SMEM),
+            pl.BlockSpec(memory_space=pltpu.VMEM),
+            pl.BlockSpec(memory_space=pltpu.SMEM),
+        ],
         out_specs=pl.BlockSpec(memory_space=pltpu.VMEM),
         scratch_shapes=[
             pltpu.VMEM((chunks, groups, n_pair, step, width), jnp.bfloat16),
@@ -347,6 +383,8 @@
             pltpu.VMEM((2, chunks * chunks, tall, tall), jnp.float32),
             pltpu.VMEM((chunks * chunks, tall, tall), jnp.float32),
             pltpu.VMEM((tall, width), jnp.bfloat16),
+            pltpu.VMEM((n_pair, 1, width // n_pair), jnp.float32),
+            pltpu.VMEM((1, width), jnp.float32),
             dma((chunks, n_pair)),
             dma((chunks, n_pair)),
             dma((chunks, n_aux, n_pair)),
@@ -358,11 +396,13 @@
             dma((chunks, 2)),
             dma((chunks,)),
             dma((chunks,)),
+            dma((n_pair,)),
+            dma((n_pair,)),
         ],
         compiler_params=pltpu.CompilerParams(
             collective_id=1, has_side_effects=True, vmem_limit_bytes=60 * 2**20
         ),
-    )(pieces, weight)
+    )(pieces, eps_occ, eps_virt[None, :], freq)
 
 
 def local(mesh, three_center, eps_occ, eps_virt, freq):
@@ -375,18 +415,8 @@
 
 def whole_kernel(n_aux, n_rep, three_center, eps_occ, eps_virt, freq):
     rows, n_pair, n_virt = three_center.shape
-    pad = -n_virt % 128
-    chunks = rows // 32
-    virt = lax.all_gather(eps_virt, "pair", axis=0, tiled=True)
-    occ = lax.dynamic_index_in_dim(eps_occ, lax.axis_index("pair"), keepdims=False)
-    excite = virt - occ
-    weight = 2.0 * excite / (excite * excite + freq[0] * freq[0])
-    weight = jnp.pad(weight, (0, pad))[None, :]
-    pieces = jnp.pad(three_center.transpose(1, 0, 2), ((0, 0), (0, 0), (0, pad)))
-    pieces = pieces.reshape(n_pair, chunks, 32, n_virt + pad)
-    out = fused(pieces, weight, n_aux, n_rep)
-    out = out.reshape(chunks, chunks, n_pair, 32, n_pair, 32)
-    return out.transpose(2, 0, 3, 4, 1, 5).reshape(n_pair * rows, n_pair * rows)
+    pieces = three_center.transpose(1, 0, 2).reshape(n_pair, rows // 32, 32, n_virt)
+    return fused(pieces, eps_occ, eps_virt, freq, n_aux, n_rep)
 
 
 def staged(n_pair, n_aux, n_rep, three_center, eps_occ, eps_virt, freq):

time: 425 us -> 376 us (0.88)
  local copies, waits for them, and re-layouts: 45 us -> 11.6 us
  blocking collectives: 12 us -> 0 us
    reshape x3 -> x0, local copies, waits for them, and re-layouts: 25.5 us -> none  [the longest x2 18 us: whole_kernel(): out = out.reshape(chunks, chunks, n_pair, 32, n_pair, 32)]
    unnamed x1 -> x0, blocking collectives: 12 us -> none
    transpose x0 -> x1, local copies, waits for them, and re-layouts: none -> 8.92 us  [whole_kernel(): three_center.transpose(1, 0, 2).reshape(n_pair, rows // 32, 32, n_virt)]
    pad x2 -> x0, local copies, waits for them, and re-layouts: 8.57 us -> none  [the longest x1 8.57 us: whole_kernel(): jnp.pad(three_center.transpose(1, 0, 2), ((0, 0), (0, 0), (0, pad)))]
    unnamed x10 -> x1, local copies, waits for them, and re-layouts: 9.72 us -> 2.7 us
    pallas_call x1, Pallas kernels: 365 us -> 361 us  [fused(): pl.pallas_call(functools.partial(fused_kernel, sizes), out_shape=jax.Shap...]
where the time goes in v3:
time: 376 us; the launch traced here: 373 us
  Pallas kernels  361 us (96%)
  local copies, waits for them, and re-layouts  11.6 us (3%)
    pallas_call x1, Pallas kernels, fused(): pl.pallas_call(functools.partial(fused_kernel, sizes), out_shape=jax.Shap...  361 us
    transpose x1, local copies, waits for them, and re-layouts, whole_kernel(): three_center.transpose(1, 0, 2).reshape(n_pair, rows // 32, 32, n_virt)  8.92 us

profile of v3, /device:TPU:25, one launch (start us, length us, event | category | flops | bytes accessed | tf_op | source)
XLA Modules:
  0.0 372.8 jit_solution(11928970684322118157)
XLA Ops:
  0.7 8.9 %copy.5 = bf16[4,160,8000]{2,1,0:T(8,128)(2,1)} copy(bf16[4,160,8000]{2,0,1:T(4,128)(2,1)} %bitcast.4) | data formatting | bytes 20480000 | tf_op jit(solution)/shard_map/transpose | solution.py:418
  9.6 360.5 %shard_map.46 = f32[640,640]{1,0:T(8,128)} custom-call(bf16[4,5,32,8000]{3,2,1,0:T(8,128)(2,1)} %bitcast.3, f32[4]{0:T(128)} %occ_ref.1, f32[1,2000]{1,0:T(1,128)} %bitcast.5, f32[1]{0:T(128)S(6)} %copy.7.freq_ref), custom_call_target="tpu_custom_call" | custom-call | tf_op jit(solution)/shard_map/pallas_call | solution.py:370
  370.1 2.7 copy.8

commit v4 on v3

--- a/solution.py
+++ b/solution.py
@@ -332,13 +332,13 @@
             for j in range(1, n_pair):
                 arrived(c, j)
             start_z(c + 2)
+        if c > 1:
+            halve(c - 2)
         if c:
             for j in range(n_pair):
                 crossed(c - 1, j)
             complete(c - 1)
             compute(c - 1)
-        if c > 1:
-            halve(c - 2)
         if c > 2:
             finish(c - 3)
     halve(chunks - 1)

time: 376 us -> 412 us (1.096)
  Pallas kernels: 361 us -> 396 us
    pallas_call x1, Pallas kernels: 361 us -> 396 us  [fused(): pl.pallas_call(functools.partial(fused_kernel, sizes), out_shape=jax.Shap...]
where the time goes in v4:
time: 412 us; the launch traced here: 408 us
  Pallas kernels  396 us (96%)
  local copies, waits for them, and re-layouts  11.6 us (3%)
    pallas_call x1, Pallas kernels, fused(): pl.pallas_call(functools.partial(fused_kernel, sizes), out_shape=jax.Shap...  396 us
    transpose x1, local copies, waits for them, and re-layouts, whole_kernel(): three_center.transpose(1, 0, 2).reshape(n_pair, rows // 32, 32, n_virt)  8.92 us

profile of v4, /device:TPU:25, one launch (start us, length us, event | category | flops | bytes accessed | tf_op | source)
XLA Modules:
  0.0 407.9 jit_solution(4138893390504967802)
XLA Ops:
  0.7 8.9 %copy.5 = bf16[4,160,8000]{2,1,0:T(8,128)(2,1)} copy(bf16[4,160,8000]{2,0,1:T(4,128)(2,1)} %bitcast.4) | data formatting | bytes 20480000 | tf_op jit(solution)/shard_map/transpose | solution.py:418
  9.6 395.6 %shard_map.46 = f32[640,640]{1,0:T(8,128)} custom-call(bf16[4,5,32,8000]{3,2,1,0:T(8,128)(2,1)} %bitcast.3, f32[4]{0:T(128)} %occ_ref.1, f32[1,2000]{1,0:T(1,128)} %bitcast.5, f32[1]{0:T(128)S(6)} %copy.7.freq_ref), custom_call_target="tpu_custom_call" | custom-call | tf_op jit(solution)/shard_map/pallas_call | solution.py:370
  405.2 2.7 copy.8
